TPU v7x, 512 devices: a whole 4x8x8 slice. The times are simulated.
512 devices in a mesh: ctx: 64 (over z_lo, y, core), tp: 8 (over z_hi, x).
Axes of the slice: x: 4, y: 8, z: 8 (z_hi: 2, z_lo: 4; z = z_hi * 4 + z_lo), core: 2. Of those that a mesh axis runs over, the one named last changes fastest.
Arguments:
- hidden_in: bfloat16 [16384, 2048], P('ctx', 'tp'), may hold values from -6 to 6
- ln_gain: float32 [2048], replicated, may hold values from 0.1 to 1.9
- ln_bias: float32 [2048], replicated, may hold values from -3 to 3
- w_qkv: bfloat16 [3, 2048, 2048], P(None, None, 'tp')
- w_out: bfloat16 [2048, 2048], P('tp'), may hold values from -0.375 to 0.375
- segment_ids: int32 [16384], P('ctx'), may hold values from 0 to 2, as said below
- prompt_lengths: int32 [3], replicated, may hold values from 1 to 8192, as said below
- page_table: int32 [3, 64], replicated, may hold values from -1 to 319, as said below
Outputs:
- attn_out: bfloat16 [16384, 2048], P('ctx', 'tp')
- kv_cache: bfloat16 [320, 128, 2, 2048], P('ctx', None, None, 'tp')
Inputs may be any that keep to these rules, and one draw needn't show every extreme that they name: `segment_ids`: each prompt's tokens are consecutive and the numbers never fall along the tokens; prompt i holds exactly prompt_lengths[i] tokens. `prompt_lengths`: the lengths sum to 16384; prompt 0 is shorter than 256 tokens and not a multiple of 128; prompt 1 is the longest, exactly 8192 tokens. `page_table`: for page j of prompt i with j * 128 below prompt_lengths[i], the entry is owner * 5 + slot with slot below 5, where owner is the ctx index whose tokens include the page's first token, starts_i + j * 128; distinct pages have distinct entries; all other entries are -1.
All inputs are finite; a program needn't handle non-finite values.
Results may differ from a plain program's by a relative error of at most 0.013.
Values may be sent and summed in bfloat16 or wider, within the bound.
A program may use at most 128 MiB of HBM per device.

v0:
```python
import math
import jax
import jax.numpy as jnp
from jax import lax
from jax.sharding import PartitionSpec as P

HD = 256
PAGE = 128
EPSILON = 1e-05


def passed_along(value, axis, steps):
    count = lax.axis_size(axis)
    first, last = (max(0, -steps), min(count, count - steps))
    return lax.ppermute(value, axis, [(source, source + steps) for source in range(first, last)])


def normalize(inputs, norm_gain, norm_bias):
    average = jnp.sum(inputs, axis=-1, keepdims=True) / inputs.shape[-1]
    centered = inputs - average
    spread = jnp.sum(centered * centered, axis=-1, keepdims=True) / inputs.shape[-1]
    return centered * lax.rsqrt(spread + EPSILON) * norm_gain + norm_bias


def rotary(inputs, positions):
    quarter = inputs.shape[-1] // 4
    halfway = quarter // 2
    exponent = jnp.arange(0, quarter, 2).astype(jnp.float32) / quarter
    inverse = jnp.power(jnp.float32(10000.0), -exponent)
    angles = positions.astype(jnp.float32)[:, None] * inverse[None, :]
    cosine_table = jnp.concatenate([jnp.cos(angles), jnp.cos(angles)], axis=-1)[:, None, :]
    sine_table = jnp.concatenate([jnp.sin(angles), jnp.sin(angles)], axis=-1)[:, None, :]
    leading = inputs[..., :quarter]
    turned = jnp.concatenate([-leading[..., halfway:], leading[..., :halfway]], axis=-1)
    return jnp.concatenate(
        [leading * cosine_table + turned * sine_table, inputs[..., quarter:]], axis=-1
    )


def segment_positions(segment_rows, row_index, starts):
    table_span = starts.shape[0]
    matches = segment_rows[:, None] == jnp.arange(table_span, dtype=jnp.int32)[None, :]
    first_rows = jnp.sum(jnp.where(matches, starts[None, :], 0), axis=1)
    return row_index - first_rows


def attend(carry_state, query_heads, pair_block, key_marks, query_marks, causal):
    running_max, running_sum, running_acc = carry_state
    scores = jnp.einsum(
        "qhd,khd->hqk", query_heads, pair_block[:, 0], preferred_element_type=jnp.float32
    ) / math.sqrt(query_heads.shape[-1])
    visible = query_marks[:, None] == key_marks[None, :]
    if causal:
        row_count = query_heads.shape[0]
        visible = visible & (jnp.arange(row_count)[None, :] <= jnp.arange(row_count)[:, None])
    scores = jnp.where(visible[None], scores, -jnp.inf)
    newest_max = jnp.maximum(running_max, jnp.max(scores, axis=-1))
    rescale = jnp.exp(running_max - newest_max)
    weights = jnp.exp(scores - newest_max[..., None]).astype(jnp.bfloat16)
    weights = lax.optimization_barrier(weights)
    running_sum = running_sum * rescale + jnp.sum(weights.astype(jnp.float32), axis=-1)
    running_acc = running_acc * rescale[..., None] + jnp.einsum(
        "hqk,khd->hqd", weights, pair_block[:, 1], preferred_element_type=jnp.float32
    )
    return (newest_max, running_sum, running_acc)


def visit_block(carry_state, query_heads, query_marks, pair_block, key_marks):
    tail_mark = key_marks[key_marks.shape[0] - 1]
    relevant = tail_mark == query_marks[0]
    return lax.cond(
        relevant,
        lambda current: attend(current, query_heads, pair_block, key_marks, query_marks, False),
        lambda current: current,
        carry_state,
    )


def per_device(hidden_in, ln_gain, ln_bias, w_qkv, w_out, segment_ids, prompt_lengths, page_table):
    token_rows = hidden_in.shape[0]
    model_width = w_out.shape[1]
    local_heads = w_out.shape[0] // HD
    my_index = lax.axis_index("ctx")
    reach = lax.axis_size("ctx") // 2
    whole_rows = lax.all_gather(hidden_in, "tp", axis=1, tiled=True)
    normed = normalize(whole_rows.astype(jnp.float32), ln_gain, ln_bias).astype(jnp.bfloat16)
    projected = jnp.einsum("td,jdh->tjh", normed, w_qkv, preferred_element_type=jnp.float32)
    starts = jnp.cumsum(prompt_lengths) - prompt_lengths
    row_index = my_index * token_rows + jnp.arange(token_rows, dtype=jnp.int32)
    positions = segment_positions(segment_ids, row_index, starts)
    query_heads = rotary(projected[:, 0].reshape(token_rows, local_heads, HD), positions).astype(
        jnp.bfloat16
    )
    key_heads = rotary(projected[:, 1].reshape(token_rows, local_heads, HD), positions).astype(
        jnp.bfloat16
    )
    value_heads = projected[:, 2].reshape(token_rows, local_heads, HD).astype(jnp.bfloat16)
    pair_block = jnp.stack([key_heads, value_heads], axis=1)
    own_marks = segment_ids + 1
    carry_state = (
        jnp.full((local_heads, token_rows), -jnp.inf, jnp.float32),
        jnp.zeros((local_heads, token_rows), jnp.float32),
        jnp.zeros((local_heads, token_rows, HD), jnp.float32),
    )
    carry_state = attend(carry_state, query_heads, pair_block, own_marks, own_marks, True)

    def relay_step(step, state):
        moving_pair, moving_marks, current = state
        moving_pair, moving_marks = passed_along((moving_pair, moving_marks), "ctx", 1)
        current = visit_block(current, query_heads, own_marks, moving_pair, moving_marks)
        return (moving_pair, moving_marks, current)

    carry_state = lax.fori_loop(0, reach, relay_step, (pair_block, own_marks, carry_state))[2]
    running_max, running_sum, running_acc = carry_state
    attended = (running_acc / running_sum[..., None]).astype(jnp.bfloat16)
    partial_value = jnp.einsum(
        "hqd,hde->qe",
        attended,
        w_out.reshape(local_heads, HD, model_width),
        preferred_element_type=jnp.float32,
    )
    attn_out = lax.psum_scatter(
        partial_value.astype(jnp.bfloat16), "tp", scatter_dimension=1, tiled=True
    )
    tail_pair, tail_marks = passed_along((pair_block[:PAGE], own_marks[:PAGE]), "ctx", -1)
    every_pair = jnp.concatenate([pair_block, tail_pair], axis=0)
    every_marks = jnp.concatenate([own_marks, tail_marks], axis=0)
    every_index = my_index * token_rows + jnp.arange(token_rows + PAGE, dtype=jnp.int32)
    every_segment = jnp.maximum(every_marks - 1, 0)
    every_position = segment_positions(every_segment, every_index, starts)
    page_number = every_position // PAGE
    page_offset = every_position % PAGE
    page_owner = (every_index - page_offset) // token_rows
    is_owned = (every_marks > 0) & (page_owner == my_index)
    page_count = page_table.shape[1]
    table_entry = jnp.take(
        page_table.reshape(-1),
        every_segment * page_count + jnp.clip(page_number, 0, page_count - 1),
    )
    kv_slots = token_rows // PAGE + 3
    target = jnp.where(is_owned, table_entry % kv_slots * PAGE + page_offset, -1)
    placing = (jnp.arange(kv_slots * PAGE, dtype=jnp.int32)[:, None] == target[None, :]).astype(
        jnp.bfloat16
    )
    flat_pair = every_pair.reshape(token_rows + PAGE, 2 * local_heads * HD)
    written = jnp.dot(placing, flat_pair, preferred_element_type=jnp.float32).astype(jnp.bfloat16)
    kv_cache = written.reshape(kv_slots, PAGE, 2, local_heads * HD)
    return (attn_out, kv_cache)


def solution(mesh):
    return jax.shard_map(
        per_device,
        mesh=mesh,
        in_specs=(P("ctx", "tp"), P(), P(), P(None, None, "tp"), P("tp", None), P("ctx"), P(), P()),
        out_specs=(P("ctx", "tp"), P("ctx", None, None, "tp")),
        check_vma=False,
    )
```

profile of v0, /device:TPU:8, one launch (start us, length us, event | category | flops | bytes accessed | tf_op | source)
XLA Modules:
  0.0 715.6 jit_solution(10139987149686012293)
XLA Ops:
  12.5 70.7 %all-gather.2.cloned.1.call-done = bf16[256,2048]{1,0:T(8,128)(2,1)} async-done(((bf16[256,256]{1,0:T(8,128)(2,1)}), bf16[256,2048]{1,0:T(8,128)(2,1)}) %all-gather.2.cloned.1.call-update) | async-done | bytes 1048592 | tf_op jit(solution)/shard_map/all_gather | solution.py:85
  95.2 446.7 %while.18 = (s32[]{:T(128)}, bf16[256,2,1,256]{3,0,2,1:T(8,128)(2,1)}, s32[256]{0:T(256)}, f32[1,256]{1,0:T(1,128)S(1)}, f32[1,256]{1,0:T(1,128)S(1)}, /*index=5...) while((s32[]{:T(128)}, bf16[256,2,1,256]{3,0,2,1:T(8,128)(2,1)}, ...), condition=%wide.region_11.12_spmd, body=%wide.region_6.11_spmd.sunk | while | flops 67764736 | bytes 3431739 | solution.py:113
  97.1 3.5 collective-permute-start.1
  105.6 3.2 conditional.2
  111.4 3.5 collective-permute-start.1
  119.9 3.2 conditional.2
  125.8 3.5 collective-permute-start.1
  135.0 4.3 collective-permute-start
  139.3 4.3 collective-permute-start.1
  147.8 2.6 collective-permute-start
  150.4 8.2 %collective-permute-start.1 = (s32[256]{0:T(256)}, s32[256]{0:T(256)S(1)}, u32[]{:S(2)}, u32[]{:S(2)}) collective-permute-start(s32[256]{0:T(256)} %get-tuple-element.206), channel_id=1, source_target_pairs={{0,8},{8,16},{16,24},{24,32},{32,40},{40,48},{48,56},{56,64},{64,7... | collective-permute-start | bytes 3080 | tf_op jit(solution)/shard_map/while/body/eval_jaxpr/ppermute | solution.py:15
  162.7 2.6 collective-permute-start
  165.3 5.5 collective-permute-start.1
  175.1 5.7 collective-permute-start
  180.8 5.6 collective-permute-start.1
  190.6 2.6 collective-permute-start
  193.2 8.8 %collective-permute-start.1 = (s32[256]{0:T(256)}, s32[256]{0:T(256)S(1)}, u32[]{:S(2)}, u32[]{:S(2)}) collective-permute-start(s32[256]{0:T(256)} %get-tuple-element.206), channel_id=1, source_target_pairs={{0,8},{8,16},{16,24},{24,32},{32,40},{40,48},{48,56},{56,64},{64,7... | collective-permute-start | bytes 3080 | tf_op jit(solution)/shard_map/while/body/eval_jaxpr/ppermute | solution.py:15
  206.2 2.6 collective-permute-start
  208.8 5.5 collective-permute-start.1
  218.5 5.6 collective-permute-start
  224.1 5.7 collective-permute-start.1
  234.0 2.6 collective-permute-start
  236.6 8.8 %collective-permute-start.1 = (s32[256]{0:T(256)}, s32[256]{0:T(256)S(1)}, u32[]{:S(2)}, u32[]{:S(2)}) collective-permute-start(s32[256]{0:T(256)} %get-tuple-element.206), channel_id=1, source_target_pairs={{0,8},{8,16},{16,24},{24,32},{32,40},{40,48},{48,56},{56,64},{64,7... | collective-permute-start | bytes 3080 | tf_op jit(solution)/shard_map/while/body/eval_jaxpr/ppermute | solution.py:15
  249.6 2.6 collective-permute-start
  252.2 5.5 collective-permute-start.1
  261.9 2.6 collective-permute-start
  264.5 5.5 collective-permute-start.1
  276.8 5.5 collective-permute-start.1
  289.2 5.5 collective-permute-start.1
  298.9 4.3 collective-permute-start
  303.2 6.8 collective-permute-start.1
  314.2 2.6 collective-permute-start
  316.8 9.7 %collective-permute-start.1 = (s32[256]{0:T(256)}, s32[256]{0:T(256)S(1)}, u32[]{:S(2)}, u32[]{:S(2)}) collective-permute-start(s32[256]{0:T(256)} %get-tuple-element.206), channel_id=1, source_target_pairs={{0,8},{8,16},{16,24},{24,32},{32,40},{40,48},{48,56},{56,64},{64,7... | collective-permute-start | bytes 3080 | tf_op jit(solution)/shard_map/while/body/eval_jaxpr/ppermute | solution.py:15
  330.6 2.6 collective-permute-start
  333.2 6.4 collective-permute-start.1
  343.8 5.3 collective-permute-start
  349.2 6.9 collective-permute-start.1
  362.9 9.7 %collective-permute-start.1 = (s32[256]{0:T(256)}, s32[256]{0:T(256)S(1)}, u32[]{:S(2)}, u32[]{:S(2)}) collective-permute-start(s32[256]{0:T(256)} %get-tuple-element.206), channel_id=1, source_target_pairs={{0,8},{8,16},{16,24},{24,32},{32,40},{40,48},{48,56},{56,64},{64,7... | collective-permute-start | bytes 3080 | tf_op jit(solution)/shard_map/while/body/eval_jaxpr/ppermute | solution.py:15
  379.3 6.4 collective-permute-start.1
  390.0 5.2 collective-permute-start
  395.2 7.0 collective-permute-start.1
  406.4 2.6 collective-permute-start
  409.0 9.7 %collective-permute-start.1 = (s32[256]{0:T(256)}, s32[256]{0:T(256)S(1)}, u32[]{:S(2)}, u32[]{:S(2)}) collective-permute-start(s32[256]{0:T(256)} %get-tuple-element.206), channel_id=1, source_target_pairs={{0,8},{8,16},{16,24},{24,32},{32,40},{40,48},{48,56},{56,64},{64,7... | collective-permute-start | bytes 3080 | tf_op jit(solution)/shard_map/while/body/eval_jaxpr/ppermute | solution.py:15
  422.9 2.6 collective-permute-start
  425.4 6.4 collective-permute-start.1
  436.1 2.6 collective-permute-start
  438.7 6.4 collective-permute-start.1
  451.9 6.4 collective-permute-start.1
  462.5 2.6 collective-permute-start
  465.1 6.4 collective-permute-start.1
  478.4 6.4 collective-permute-start.1
  489.0 2.6 collective-permute-start
  491.6 6.4 collective-permute-start.1
  502.2 2.6 collective-permute-start
  504.8 6.4 collective-permute-start.1
  518.0 6.4 collective-permute-start.1
  528.7 2.6 collective-permute-start
  531.3 6.4 collective-permute-start.1
  541.9 2.8 convolution_convert_fusion
  548.9 3.9 gather_fusion
  552.9 3.6 collective-permute-start.3
  557.2 3.6 collective-permute-done.3
  563.1 2.7 reshape.659
  565.8 143.0 %reduce-scatter.2.cloned.1.call-done = bf16[256,256]{1,0:T(8,128)(2,1)} async-done(((bf16[256,2048]{1,0:T(8,128)(2,1)}), bf16[256,256]{1,0:T(8,128)(2,1)}) %reduce-scatter.2.cloned.1.call-update) | async-done | bytes 131088 | tf_op jit(solution)/shard_map/reduce_scatter | solution.py:122
  (313 shorter events, 153.2 us)
Async XLA Ops:
  7.2 75.9 %all-gather.2.cloned.1.call-start = ((), (), s32[]{:S(2)}) async-start(), calls=%async_computation.1 | async-start | bytes 1179648 | tf_op jit(solution)/shard_map/all_gather | solution.py:85
  7.9 700.9 %reduce-scatter.2.cloned.1.call-start = ((), (), s32[]{:S(2)}) async-start(), calls=%async_computation.2 | async-start | bytes 1179648 | tf_op jit(solution)/shard_map/reduce_scatter | solution.py:122
  95.2 10.4 %collective-permute-start = (bf16[256,2,1,256]{3,0,2,1:T(8,128)(2,1)}, bf16[256,2,1,256]{3,0,2,1:T(8,128)(2,1)S(1)}, u32[]{:S(2)}, u32[]{:S(2)}) collective-permute-start(bf16[256,2,1,256]{3,0,2,1:T(8,128)(2,1)} %get-tuple-element.205), channel_id=1, source_target_pairs={{0,8},{8,16},{16,24},{24,32},{32,40},{40,48},{48,56},{56,64},{64,7... | collective-permute-start | bytes 786440 | tf_op jit(solution)/shard_map/while/body/eval_jaxpr/ppermute | solution.py:15
  97.1 6.0 collective-permute-start.1
  109.5 10.4 %collective-permute-start = (bf16[256,2,1,256]{3,0,2,1:T(8,128)(2,1)}, bf16[256,2,1,256]{3,0,2,1:T(8,128)(2,1)S(1)}, u32[]{:S(2)}, u32[]{:S(2)}) collective-permute-start(bf16[256,2,1,256]{3,0,2,1:T(8,128)(2,1)} %get-tuple-element.205), channel_id=1, source_target_pairs={{0,8},{8,16},{16,24},{24,32},{32,40},{40,48},{48,56},{56,64},{64,7... | collective-permute-start | bytes 786440 | tf_op jit(solution)/shard_map/while/body/eval_jaxpr/ppermute | solution.py:15
  123.9 10.4 %collective-permute-start = (bf16[256,2,1,256]{3,0,2,1:T(8,128)(2,1)}, bf16[256,2,1,256]{3,0,2,1:T(8,128)(2,1)S(1)}, u32[]{:S(2)}, u32[]{:S(2)}) collective-permute-start(bf16[256,2,1,256]{3,0,2,1:T(8,128)(2,1)} %get-tuple-element.205), channel_id=1, source_target_pairs={{0,8},{8,16},{16,24},{24,32},{32,40},{40,48},{48,56},{56,64},{64,7... | collective-permute-start | bytes 786440 | tf_op jit(solution)/shard_map/while/body/eval_jaxpr/ppermute | solution.py:15
  135.0 12.1 %collective-permute-start = (bf16[256,2,1,256]{3,0,2,1:T(8,128)(2,1)}, bf16[256,2,1,256]{3,0,2,1:T(8,128)(2,1)S(1)}, u32[]{:S(2)}, u32[]{:S(2)}) collective-permute-start(bf16[256,2,1,256]{3,0,2,1:T(8,128)(2,1)} %get-tuple-element.205), channel_id=1, source_target_pairs={{0,8},{8,16},{16,24},{24,32},{32,40},{40,48},{48,56},{56,64},{64,7... | collective-permute-start | bytes 786440 | tf_op jit(solution)/shard_map/while/body/eval_jaxpr/ppermute | solution.py:15
  147.8 14.2 %collective-permute-start = (bf16[256,2,1,256]{3,0,2,1:T(8,128)(2,1)}, bf16[256,2,1,256]{3,0,2,1:T(8,128)(2,1)S(1)}, u32[]{:S(2)}, u32[]{:S(2)}) collective-permute-start(bf16[256,2,1,256]{3,0,2,1:T(8,128)(2,1)} %get-tuple-element.205), channel_id=1, source_target_pairs={{0,8},{8,16},{16,24},{24,32},{32,40},{40,48},{48,56},{56,64},{64,7... | collective-permute-start | bytes 786440 | tf_op jit(solution)/shard_map/while/body/eval_jaxpr/ppermute | solution.py:15
  150.4 9.2 %collective-permute-start.1 = (s32[256]{0:T(256)}, s32[256]{0:T(256)S(1)}, u32[]{:S(2)}, u32[]{:S(2)}) collective-permute-start(s32[256]{0:T(256)} %get-tuple-element.206), channel_id=1, source_target_pairs={{0,8},{8,16},{16,24},{24,32},{32,40},{40,48},{48,56},{56,64},{64,7... | collective-permute-start | bytes 3080 | tf_op jit(solution)/shard_map/while/body/eval_jaxpr/ppermute | solution.py:15
  162.7 11.6 %collective-permute-start = (bf16[256,2,1,256]{3,0,2,1:T(8,128)(2,1)}, bf16[256,2,1,256]{3,0,2,1:T(8,128)(2,1)S(1)}, u32[]{:S(2)}, u32[]{:S(2)}) collective-permute-start(bf16[256,2,1,256]{3,0,2,1:T(8,128)(2,1)} %get-tuple-element.205), channel_id=1, source_target_pairs={{0,8},{8,16},{16,24},{24,32},{32,40},{40,48},{48,56},{56,64},{64,7... | collective-permute-start | bytes 786440 | tf_op jit(solution)/shard_map/while/body/eval_jaxpr/ppermute | solution.py:15
  165.3 6.6 collective-permute-start.1
  175.1 14.8 %collective-permute-start = (bf16[256,2,1,256]{3,0,2,1:T(8,128)(2,1)}, bf16[256,2,1,256]{3,0,2,1:T(8,128)(2,1)S(1)}, u32[]{:S(2)}, u32[]{:S(2)}) collective-permute-start(bf16[256,2,1,256]{3,0,2,1:T(8,128)(2,1)} %get-tuple-element.205), channel_id=1, source_target_pairs={{0,8},{8,16},{16,24},{24,32},{32,40},{40,48},{48,56},{56,64},{64,7... | collective-permute-start | bytes 786440 | tf_op jit(solution)/shard_map/while/body/eval_jaxpr/ppermute | solution.py:15
  180.8 6.7 collective-permute-start.1
  190.6 14.8 %collective-permute-start = (bf16[256,2,1,256]{3,0,2,1:T(8,128)(2,1)}, bf16[256,2,1,256]{3,0,2,1:T(8,128)(2,1)S(1)}, u32[]{:S(2)}, u32[]{:S(2)}) collective-permute-start(bf16[256,2,1,256]{3,0,2,1:T(8,128)(2,1)} %get-tuple-element.205), channel_id=1, source_target_pairs={{0,8},{8,16},{16,24},{24,32},{32,40},{40,48},{48,56},{56,64},{64,7... | collective-permute-start | bytes 786440 | tf_op jit(solution)/shard_map/while/body/eval_jaxpr/ppermute | solution.py:15
  193.2 9.8 %collective-permute-start.1 = (s32[256]{0:T(256)}, s32[256]{0:T(256)S(1)}, u32[]{:S(2)}, u32[]{:S(2)}) collective-permute-start(s32[256]{0:T(256)} %get-tuple-element.206), channel_id=1, source_target_pairs={{0,8},{8,16},{16,24},{24,32},{32,40},{40,48},{48,56},{56,64},{64,7... | collective-permute-start | bytes 3080 | tf_op jit(solution)/shard_map/while/body/eval_jaxpr/ppermute | solution.py:15
  206.2 11.6 %collective-permute-start = (bf16[256,2,1,256]{3,0,2,1:T(8,128)(2,1)}, bf16[256,2,1,256]{3,0,2,1:T(8,128)(2,1)S(1)}, u32[]{:S(2)}, u32[]{:S(2)}) collective-permute-start(bf16[256,2,1,256]{3,0,2,1:T(8,128)(2,1)} %get-tuple-element.205), channel_id=1, source_target_pairs={{0,8},{8,16},{16,24},{24,32},{32,40},{40,48},{48,56},{56,64},{64,7... | collective-permute-start | bytes 786440 | tf_op jit(solution)/shard_map/while/body/eval_jaxpr/ppermute | solution.py:15
  208.8 6.6 collective-permute-start.1
  218.5 14.8 %collective-permute-start = (bf16[256,2,1,256]{3,0,2,1:T(8,128)(2,1)}, bf16[256,2,1,256]{3,0,2,1:T(8,128)(2,1)S(1)}, u32[]{:S(2)}, u32[]{:S(2)}) collective-permute-start(bf16[256,2,1,256]{3,0,2,1:T(8,128)(2,1)} %get-tuple-element.205), channel_id=1, source_target_pairs={{0,8},{8,16},{16,24},{24,32},{32,40},{40,48},{48,56},{56,64},{64,7... | collective-permute-start | bytes 786440 | tf_op jit(solution)/shard_map/while/body/eval_jaxpr/ppermute | solution.py:15
  224.1 6.7 collective-permute-start.1
  234.0 14.8 %collective-permute-start = (bf16[256,2,1,256]{3,0,2,1:T(8,128)(2,1)}, bf16[256,2,1,256]{3,0,2,1:T(8,128)(2,1)S(1)}, u32[]{:S(2)}, u32[]{:S(2)}) collective-permute-start(bf16[256,2,1,256]{3,0,2,1:T(8,128)(2,1)} %get-tuple-element.205), channel_id=1, source_target_pairs={{0,8},{8,16},{16,24},{24,32},{32,40},{40,48},{48,56},{56,64},{64,7... | collective-permute-start | bytes 786440 | tf_op jit(solution)/shard_map/while/body/eval_jaxpr/ppermute | solution.py:15
  236.6 9.8 %collective-permute-start.1 = (s32[256]{0:T(256)}, s32[256]{0:T(256)S(1)}, u32[]{:S(2)}, u32[]{:S(2)}) collective-permute-start(s32[256]{0:T(256)} %get-tuple-element.206), channel_id=1, source_target_pairs={{0,8},{8,16},{16,24},{24,32},{32,40},{40,48},{48,56},{56,64},{64,7... | collective-permute-start | bytes 3080 | tf_op jit(solution)/shard_map/while/body/eval_jaxpr/ppermute | solution.py:15
  249.6 11.6 %collective-permute-start = (bf16[256,2,1,256]{3,0,2,1:T(8,128)(2,1)}, bf16[256,2,1,256]{3,0,2,1:T(8,128)(2,1)S(1)}, u32[]{:S(2)}, u32[]{:S(2)}) collective-permute-start(bf16[256,2,1,256]{3,0,2,1:T(8,128)(2,1)} %get-tuple-element.205), channel_id=1, source_target_pairs={{0,8},{8,16},{16,24},{24,32},{32,40},{40,48},{48,56},{56,64},{64,7... | collective-permute-start | bytes 786440 | tf_op jit(solution)/shard_map/while/body/eval_jaxpr/ppermute | solution.py:15
  252.2 6.6 collective-permute-start.1
  261.9 11.6 %collective-permute-start = (bf16[256,2,1,256]{3,0,2,1:T(8,128)(2,1)}, bf16[256,2,1,256]{3,0,2,1:T(8,128)(2,1)S(1)}, u32[]{:S(2)}, u32[]{:S(2)}) collective-permute-start(bf16[256,2,1,256]{3,0,2,1:T(8,128)(2,1)} %get-tuple-element.205), channel_id=1, source_target_pairs={{0,8},{8,16},{16,24},{24,32},{32,40},{40,48},{48,56},{56,64},{64,7... | collective-permute-start | bytes 786440 | tf_op jit(solution)/shard_map/while/body/eval_jaxpr/ppermute | solution.py:15
  264.5 6.6 collective-permute-start.1
  274.2 11.6 %collective-permute-start = (bf16[256,2,1,256]{3,0,2,1:T(8,128)(2,1)}, bf16[256,2,1,256]{3,0,2,1:T(8,128)(2,1)S(1)}, u32[]{:S(2)}, u32[]{:S(2)}) collective-permute-start(bf16[256,2,1,256]{3,0,2,1:T(8,128)(2,1)} %get-tuple-element.205), channel_id=1, source_target_pairs={{0,8},{8,16},{16,24},{24,32},{32,40},{40,48},{48,56},{56,64},{64,7... | collective-permute-start | bytes 786440 | tf_op jit(solution)/shard_map/while/body/eval_jaxpr/ppermute | solution.py:15
  276.8 6.6 collective-permute-start.1
  286.6 11.6 %collective-permute-start = (bf16[256,2,1,256]{3,0,2,1:T(8,128)(2,1)}, bf16[256,2,1,256]{3,0,2,1:T(8,128)(2,1)S(1)}, u32[]{:S(2)}, u32[]{:S(2)}) collective-permute-start(bf16[256,2,1,256]{3,0,2,1:T(8,128)(2,1)} %get-tuple-element.205), channel_id=1, source_target_pairs={{0,8},{8,16},{16,24},{24,32},{32,40},{40,48},{48,56},{56,64},{64,7... | collective-permute-start | bytes 786440 | tf_op jit(solution)/shard_map/while/body/eval_jaxpr/ppermute | solution.py:15
  289.2 6.6 collective-permute-start.1
  298.9 14.6 %collective-permute-start = (bf16[256,2,1,256]{3,0,2,1:T(8,128)(2,1)}, bf16[256,2,1,256]{3,0,2,1:T(8,128)(2,1)S(1)}, u32[]{:S(2)}, u32[]{:S(2)}) collective-permute-start(bf16[256,2,1,256]{3,0,2,1:T(8,128)(2,1)} %get-tuple-element.205), channel_id=1, source_target_pairs={{0,8},{8,16},{16,24},{24,32},{32,40},{40,48},{48,56},{56,64},{64,7... | collective-permute-start | bytes 786440 | tf_op jit(solution)/shard_map/while/body/eval_jaxpr/ppermute | solution.py:15
  303.2 7.8 %collective-permute-start.1 = (s32[256]{0:T(256)}, s32[256]{0:T(256)S(1)}, u32[]{:S(2)}, u32[]{:S(2)}) collective-permute-start(s32[256]{0:T(256)} %get-tuple-element.206), channel_id=1, source_target_pairs={{0,8},{8,16},{16,24},{24,32},{32,40},{40,48},{48,56},{56,64},{64,7... | collective-permute-start | bytes 3080 | tf_op jit(solution)/shard_map/while/body/eval_jaxpr/ppermute | solution.py:15
  314.2 15.7 %collective-permute-start = (bf16[256,2,1,256]{3,0,2,1:T(8,128)(2,1)}, bf16[256,2,1,256]{3,0,2,1:T(8,128)(2,1)S(1)}, u32[]{:S(2)}, u32[]{:S(2)}) collective-permute-start(bf16[256,2,1,256]{3,0,2,1:T(8,128)(2,1)} %get-tuple-element.205), channel_id=1, source_target_pairs={{0,8},{8,16},{16,24},{24,32},{32,40},{40,48},{48,56},{56,64},{64,7... | collective-permute-start | bytes 786440 | tf_op jit(solution)/shard_map/while/body/eval_jaxpr/ppermute | solution.py:15
  316.8 10.7 %collective-permute-start.1 = (s32[256]{0:T(256)}, s32[256]{0:T(256)S(1)}, u32[]{:S(2)}, u32[]{:S(2)}) collective-permute-start(s32[256]{0:T(256)} %get-tuple-element.206), channel_id=1, source_target_pairs={{0,8},{8,16},{16,24},{24,32},{32,40},{40,48},{48,56},{56,64},{64,7... | collective-permute-start | bytes 3080 | tf_op jit(solution)/shard_map/while/body/eval_jaxpr/ppermute | solution.py:15
  330.6 12.5 %collective-permute-start = (bf16[256,2,1,256]{3,0,2,1:T(8,128)(2,1)}, bf16[256,2,1,256]{3,0,2,1:T(8,128)(2,1)S(1)}, u32[]{:S(2)}, u32[]{:S(2)}) collective-permute-start(bf16[256,2,1,256]{3,0,2,1:T(8,128)(2,1)} %get-tuple-element.205), channel_id=1, source_target_pairs={{0,8},{8,16},{16,24},{24,32},{32,40},{40,48},{48,56},{56,64},{64,7... | collective-permute-start | bytes 786440 | tf_op jit(solution)/shard_map/while/body/eval_jaxpr/ppermute | solution.py:15
  333.2 7.5 %collective-permute-start.1 = (s32[256]{0:T(256)}, s32[256]{0:T(256)S(1)}, u32[]{:S(2)}, u32[]{:S(2)}) collective-permute-start(s32[256]{0:T(256)} %get-tuple-element.206), channel_id=1, source_target_pairs={{0,8},{8,16},{16,24},{24,32},{32,40},{40,48},{48,56},{56,64},{64,7... | collective-permute-start | bytes 3080 | tf_op jit(solution)/shard_map/while/body/eval_jaxpr/ppermute | solution.py:15
  343.8 15.7 %collective-permute-start = (bf16[256,2,1,256]{3,0,2,1:T(8,128)(2,1)}, bf16[256,2,1,256]{3,0,2,1:T(8,128)(2,1)S(1)}, u32[]{:S(2)}, u32[]{:S(2)}) collective-permute-start(bf16[256,2,1,256]{3,0,2,1:T(8,128)(2,1)} %get-tuple-element.205), channel_id=1, source_target_pairs={{0,8},{8,16},{16,24},{24,32},{32,40},{40,48},{48,56},{56,64},{64,7... | collective-permute-start | bytes 786440 | tf_op jit(solution)/shard_map/while/body/eval_jaxpr/ppermute | solution.py:15
  349.2 7.9 %collective-permute-start.1 = (s32[256]{0:T(256)}, s32[256]{0:T(256)S(1)}, u32[]{:S(2)}, u32[]{:S(2)}) collective-permute-start(s32[256]{0:T(256)} %get-tuple-element.206), channel_id=1, source_target_pairs={{0,8},{8,16},{16,24},{24,32},{32,40},{40,48},{48,56},{56,64},{64,7... | collective-permute-start | bytes 3080 | tf_op jit(solution)/shard_map/while/body/eval_jaxpr/ppermute | solution.py:15
  360.3 15.7 %collective-permute-start = (bf16[256,2,1,256]{3,0,2,1:T(8,128)(2,1)}, bf16[256,2,1,256]{3,0,2,1:T(8,128)(2,1)S(1)}, u32[]{:S(2)}, u32[]{:S(2)}) collective-permute-start(bf16[256,2,1,256]{3,0,2,1:T(8,128)(2,1)} %get-tuple-element.205), channel_id=1, source_target_pairs={{0,8},{8,16},{16,24},{24,32},{32,40},{40,48},{48,56},{56,64},{64,7... | collective-permute-start | bytes 786440 | tf_op jit(solution)/shard_map/while/body/eval_jaxpr/ppermute | solution.py:15
  362.9 10.7 %collective-permute-start.1 = (s32[256]{0:T(256)}, s32[256]{0:T(256)S(1)}, u32[]{:S(2)}, u32[]{:S(2)}) collective-permute-start(s32[256]{0:T(256)} %get-tuple-element.206), channel_id=1, source_target_pairs={{0,8},{8,16},{16,24},{24,32},{32,40},{40,48},{48,56},{56,64},{64,7... | collective-permute-start | bytes 3080 | tf_op jit(solution)/shard_map/while/body/eval_jaxpr/ppermute | solution.py:15
  376.7 12.5 %collective-permute-start = (bf16[256,2,1,256]{3,0,2,1:T(8,128)(2,1)}, bf16[256,2,1,256]{3,0,2,1:T(8,128)(2,1)S(1)}, u32[]{:S(2)}, u32[]{:S(2)}) collective-permute-start(bf16[256,2,1,256]{3,0,2,1:T(8,128)(2,1)} %get-tuple-element.205), channel_id=1, source_target_pairs={{0,8},{8,16},{16,24},{24,32},{32,40},{40,48},{48,56},{56,64},{64,7... | collective-permute-start | bytes 786440 | tf_op jit(solution)/shard_map/while/body/eval_jaxpr/ppermute | solution.py:15
  379.3 7.5 %collective-permute-start.1 = (s32[256]{0:T(256)}, s32[256]{0:T(256)S(1)}, u32[]{:S(2)}, u32[]{:S(2)}) collective-permute-start(s32[256]{0:T(256)} %get-tuple-element.206), channel_id=1, source_target_pairs={{0,8},{8,16},{16,24},{24,32},{32,40},{40,48},{48,56},{56,64},{64,7... | collective-permute-start | bytes 3080 | tf_op jit(solution)/shard_map/while/body/eval_jaxpr/ppermute | solution.py:15
  390.0 15.7 %collective-permute-start = (bf16[256,2,1,256]{3,0,2,1:T(8,128)(2,1)}, bf16[256,2,1,256]{3,0,2,1:T(8,128)(2,1)S(1)}, u32[]{:S(2)}, u32[]{:S(2)}) collective-permute-start(bf16[256,2,1,256]{3,0,2,1:T(8,128)(2,1)} %get-tuple-element.205), channel_id=1, source_target_pairs={{0,8},{8,16},{16,24},{24,32},{32,40},{40,48},{48,56},{56,64},{64,7... | collective-permute-start | bytes 786440 | tf_op jit(solution)/shard_map/while/body/eval_jaxpr/ppermute | solution.py:15
  395.2 8.0 %collective-permute-start.1 = (s32[256]{0:T(256)}, s32[256]{0:T(256)S(1)}, u32[]{:S(2)}, u32[]{:S(2)}) collective-permute-start(s32[256]{0:T(256)} %get-tuple-element.206), channel_id=1, source_target_pairs={{0,8},{8,16},{16,24},{24,32},{32,40},{40,48},{48,56},{56,64},{64,7... | collective-permute-start | bytes 3080 | tf_op jit(solution)/shard_map/while/body/eval_jaxpr/ppermute | solution.py:15
  406.4 15.7 %collective-permute-start = (bf16[256,2,1,256]{3,0,2,1:T(8,128)(2,1)}, bf16[256,2,1,256]{3,0,2,1:T(8,128)(2,1)S(1)}, u32[]{:S(2)}, u32[]{:S(2)}) collective-permute-start(bf16[256,2,1,256]{3,0,2,1:T(8,128)(2,1)} %get-tuple-element.205), channel_id=1, source_target_pairs={{0,8},{8,16},{16,24},{24,32},{32,40},{40,48},{48,56},{56,64},{64,7... | collective-permute-start | bytes 786440 | tf_op jit(solution)/shard_map/while/body/eval_jaxpr/ppermute | solution.py:15
  409.0 10.7 %collective-permute-start.1 = (s32[256]{0:T(256)}, s32[256]{0:T(256)S(1)}, u32[]{:S(2)}, u32[]{:S(2)}) collective-permute-start(s32[256]{0:T(256)} %get-tuple-element.206), channel_id=1, source_target_pairs={{0,8},{8,16},{16,24},{24,32},{32,40},{40,48},{48,56},{56,64},{64,7... | collective-permute-start | bytes 3080 | tf_op jit(solution)/shard_map/while/body/eval_jaxpr/ppermute | solution.py:15
  422.9 12.5 %collective-permute-start = (bf16[256,2,1,256]{3,0,2,1:T(8,128)(2,1)}, bf16[256,2,1,256]{3,0,2,1:T(8,128)(2,1)S(1)}, u32[]{:S(2)}, u32[]{:S(2)}) collective-permute-start(bf16[256,2,1,256]{3,0,2,1:T(8,128)(2,1)} %get-tuple-element.205), channel_id=1, source_target_pairs={{0,8},{8,16},{16,24},{24,32},{32,40},{40,48},{48,56},{56,64},{64,7... | collective-permute-start | bytes 786440 | tf_op jit(solution)/shard_map/while/body/eval_jaxpr/ppermute | solution.py:15
  425.4 7.5 %collective-permute-start.1 = (s32[256]{0:T(256)}, s32[256]{0:T(256)S(1)}, u32[]{:S(2)}, u32[]{:S(2)}) collective-permute-start(s32[256]{0:T(256)} %get-tuple-element.206), channel_id=1, source_target_pairs={{0,8},{8,16},{16,24},{24,32},{32,40},{40,48},{48,56},{56,64},{64,7... | collective-permute-start | bytes 3080 | tf_op jit(solution)/shard_map/while/body/eval_jaxpr/ppermute | solution.py:15
  436.1 12.5 %collective-permute-start = (bf16[256,2,1,256]{3,0,2,1:T(8,128)(2,1)}, bf16[256,2,1,256]{3,0,2,1:T(8,128)(2,1)S(1)}, u32[]{:S(2)}, u32[]{:S(2)}) collective-permute-start(bf16[256,2,1,256]{3,0,2,1:T(8,128)(2,1)} %get-tuple-element.205), channel_id=1, source_target_pairs={{0,8},{8,16},{16,24},{24,32},{32,40},{40,48},{48,56},{56,64},{64,7... | collective-permute-start | bytes 786440 | tf_op jit(solution)/shard_map/while/body/eval_jaxpr/ppermute | solution.py:15
  438.7 7.5 %collective-permute-start.1 = (s32[256]{0:T(256)}, s32[256]{0:T(256)S(1)}, u32[]{:S(2)}, u32[]{:S(2)}) collective-permute-start(s32[256]{0:T(256)} %get-tuple-element.206), channel_id=1, source_target_pairs={{0,8},{8,16},{16,24},{24,32},{32,40},{40,48},{48,56},{56,64},{64,7... | collective-permute-start | bytes 3080 | tf_op jit(solution)/shard_map/while/body/eval_jaxpr/ppermute | solution.py:15
  449.3 12.5 %collective-permute-start = (bf16[256,2,1,256]{3,0,2,1:T(8,128)(2,1)}, bf16[256,2,1,256]{3,0,2,1:T(8,128)(2,1)S(1)}, u32[]{:S(2)}, u32[]{:S(2)}) collective-permute-start(bf16[256,2,1,256]{3,0,2,1:T(8,128)(2,1)} %get-tuple-element.205), channel_id=1, source_target_pairs={{0,8},{8,16},{16,24},{24,32},{32,40},{40,48},{48,56},{56,64},{64,7... | collective-permute-start | bytes 786440 | tf_op jit(solution)/shard_map/while/body/eval_jaxpr/ppermute | solution.py:15
  451.9 7.5 %collective-permute-start.1 = (s32[256]{0:T(256)}, s32[256]{0:T(256)S(1)}, u32[]{:S(2)}, u32[]{:S(2)}) collective-permute-start(s32[256]{0:T(256)} %get-tuple-element.206), channel_id=1, source_target_pairs={{0,8},{8,16},{16,24},{24,32},{32,40},{40,48},{48,56},{56,64},{64,7... | collective-permute-start | bytes 3080 | tf_op jit(solution)/shard_map/while/body/eval_jaxpr/ppermute | solution.py:15
  462.5 12.5 %collective-permute-start = (bf16[256,2,1,256]{3,0,2,1:T(8,128)(2,1)}, bf16[256,2,1,256]{3,0,2,1:T(8,128)(2,1)S(1)}, u32[]{:S(2)}, u32[]{:S(2)}) collective-permute-start(bf16[256,2,1,256]{3,0,2,1:T(8,128)(2,1)} %get-tuple-element.205), channel_id=1, source_target_pairs={{0,8},{8,16},{16,24},{24,32},{32,40},{40,48},{48,56},{56,64},{64,7... | collective-permute-start | bytes 786440 | tf_op jit(solution)/shard_map/while/body/eval_jaxpr/ppermute | solution.py:15
  465.1 7.5 %collective-permute-start.1 = (s32[256]{0:T(256)}, s32[256]{0:T(256)S(1)}, u32[]{:S(2)}, u32[]{:S(2)}) collective-permute-start(s32[256]{0:T(256)} %get-tuple-element.206), channel_id=1, source_target_pairs={{0,8},{8,16},{16,24},{24,32},{32,40},{40,48},{48,56},{56,64},{64,7... | collective-permute-start | bytes 3080 | tf_op jit(solution)/shard_map/while/body/eval_jaxpr/ppermute | solution.py:15
  475.8 12.5 %collective-permute-start = (bf16[256,2,1,256]{3,0,2,1:T(8,128)(2,1)}, bf16[256,2,1,256]{3,0,2,1:T(8,128)(2,1)S(1)}, u32[]{:S(2)}, u32[]{:S(2)}) collective-permute-start(bf16[256,2,1,256]{3,0,2,1:T(8,128)(2,1)} %get-tuple-element.205), channel_id=1, source_target_pairs={{0,8},{8,16},{16,24},{24,32},{32,40},{40,48},{48,56},{56,64},{64,7... | collective-permute-start | bytes 786440 | tf_op jit(solution)/shard_map/while/body/eval_jaxpr/ppermute | solution.py:15
  478.4 7.5 %collective-permute-start.1 = (s32[256]{0:T(256)}, s32[256]{0:T(256)S(1)}, u32[]{:S(2)}, u32[]{:S(2)}) collective-permute-start(s32[256]{0:T(256)} %get-tuple-element.206), channel_id=1, source_target_pairs={{0,8},{8,16},{16,24},{24,32},{32,40},{40,48},{48,56},{56,64},{64,7... | collective-permute-start | bytes 3080 | tf_op jit(solution)/shard_map/while/body/eval_jaxpr/ppermute | solution.py:15
  489.0 12.5 %collective-permute-start = (bf16[256,2,1,256]{3,0,2,1:T(8,128)(2,1)}, bf16[256,2,1,256]{3,0,2,1:T(8,128)(2,1)S(1)}, u32[]{:S(2)}, u32[]{:S(2)}) collective-permute-start(bf16[256,2,1,256]{3,0,2,1:T(8,128)(2,1)} %get-tuple-element.205), channel_id=1, source_target_pairs={{0,8},{8,16},{16,24},{24,32},{32,40},{40,48},{48,56},{56,64},{64,7... | collective-permute-start | bytes 786440 | tf_op jit(solution)/shard_map/while/body/eval_jaxpr/ppermute | solution.py:15
  491.6 7.5 %collective-permute-start.1 = (s32[256]{0:T(256)}, s32[256]{0:T(256)S(1)}, u32[]{:S(2)}, u32[]{:S(2)}) collective-permute-start(s32[256]{0:T(256)} %get-tuple-element.206), channel_id=1, source_target_pairs={{0,8},{8,16},{16,24},{24,32},{32,40},{40,48},{48,56},{56,64},{64,7... | collective-permute-start | bytes 3080 | tf_op jit(solution)/shard_map/while/body/eval_jaxpr/ppermute | solution.py:15
  502.2 12.5 %collective-permute-start = (bf16[256,2,1,256]{3,0,2,1:T(8,128)(2,1)}, bf16[256,2,1,256]{3,0,2,1:T(8,128)(2,1)S(1)}, u32[]{:S(2)}, u32[]{:S(2)}) collective-permute-start(bf16[256,2,1,256]{3,0,2,1:T(8,128)(2,1)} %get-tuple-element.205), channel_id=1, source_target_pairs={{0,8},{8,16},{16,24},{24,32},{32,40},{40,48},{48,56},{56,64},{64,7... | collective-permute-start | bytes 786440 | tf_op jit(solution)/shard_map/while/body/eval_jaxpr/ppermute | solution.py:15
  504.8 7.5 %collective-permute-start.1 = (s32[256]{0:T(256)}, s32[256]{0:T(256)S(1)}, u32[]{:S(2)}, u32[]{:S(2)}) collective-permute-start(s32[256]{0:T(256)} %get-tuple-element.206), channel_id=1, source_target_pairs={{0,8},{8,16},{16,24},{24,32},{32,40},{40,48},{48,56},{56,64},{64,7... | collective-permute-start | bytes 3080 | tf_op jit(solution)/shard_map/while/body/eval_jaxpr/ppermute | solution.py:15
  515.4 12.5 %collective-permute-start = (bf16[256,2,1,256]{3,0,2,1:T(8,128)(2,1)}, bf16[256,2,1,256]{3,0,2,1:T(8,128)(2,1)S(1)}, u32[]{:S(2)}, u32[]{:S(2)}) collective-permute-start(bf16[256,2,1,256]{3,0,2,1:T(8,128)(2,1)} %get-tuple-element.205), channel_id=1, source_target_pairs={{0,8},{8,16},{16,24},{24,32},{32,40},{40,48},{48,56},{56,64},{64,7... | collective-permute-start | bytes 786440 | tf_op jit(solution)/shard_map/while/body/eval_jaxpr/ppermute | solution.py:15
  518.0 7.5 %collective-permute-start.1 = (s32[256]{0:T(256)}, s32[256]{0:T(256)S(1)}, u32[]{:S(2)}, u32[]{:S(2)}) collective-permute-start(s32[256]{0:T(256)} %get-tuple-element.206), channel_id=1, source_target_pairs={{0,8},{8,16},{16,24},{24,32},{32,40},{40,48},{48,56},{56,64},{64,7... | collective-permute-start | bytes 3080 | tf_op jit(solution)/shard_map/while/body/eval_jaxpr/ppermute | solution.py:15
  528.7 12.5 %collective-permute-start = (bf16[256,2,1,256]{3,0,2,1:T(8,128)(2,1)}, bf16[256,2,1,256]{3,0,2,1:T(8,128)(2,1)S(1)}, u32[]{:S(2)}, u32[]{:S(2)}) collective-permute-start(bf16[256,2,1,256]{3,0,2,1:T(8,128)(2,1)} %get-tuple-element.205), channel_id=1, source_target_pairs={{0,8},{8,16},{16,24},{24,32},{32,40},{40,48},{48,56},{56,64},{64,7... | collective-permute-start | bytes 786440 | tf_op jit(solution)/shard_map/while/body/eval_jaxpr/ppermute | solution.py:15
  531.3 7.5 %collective-permute-start.1 = (s32[256]{0:T(256)}, s32[256]{0:T(256)S(1)}, u32[]{:S(2)}, u32[]{:S(2)}) collective-permute-start(s32[256]{0:T(256)} %get-tuple-element.206), channel_id=1, source_target_pairs={{0,8},{8,16},{16,24},{24,32},{32,40},{40,48},{48,56},{56,64},{64,7... | collective-permute-start | bytes 3080 | tf_op jit(solution)/shard_map/while/body/eval_jaxpr/ppermute | solution.py:15
  552.9 7.9 %collective-permute-start.3 = (bf16[128,2,1,256]{0,3,2,1:T(8,128)(2,1)S(1)}, bf16[128,2,1,256]{0,3,2,1:T(8,128)(2,1)S(1)}, u32[]{:S(2)}, u32[]{:S(2)}) collective-permute-start(bf16[128,2,1,256]{0,3,2,1:T(8,128)(2,1)S(1)} %slice.78), channel_id=1, source_target_pairs={{8,0},{16,8},{24,16},{32,24},{40,32},{48,40},{56,48},{64,56},{72,6... | collective-permute-start | bytes 393224 | tf_op jit(solution)/shard_map/ppermute | solution.py:15
  (16 other events, 281.2 us)
Sparse Core Ops, SparseCore 0:
  11.1 72.0 all-gather.1
  544.8 163.9 reduce-scatter.1
where the time goes:
time: 720 us; the launch traced here: 716 us
  starting transfers between devices  307 us (43%)
  waiting for transfers between devices  239 us (33%)
  local copies, waits for them, and re-layouts  89.6 us (12%)
  loops' own time  40.4 us (6%)
  matrix products  15 us (2%)
  between operations  14.2 us (2%)
  other arithmetic  10.1 us (1%)
    ppermute x66, starting transfers between devices, passed_along(): lax.ppermute(value, axis, [(source, source + steps) for source in range(f...  307 us
    reduce_scatter x1, waiting for transfers between devices, per_device(): lax.psum_scatter(partial_value.astype(jnp.bfloat16), 'tp', scatter_dimens...  143 us
    all_gather x1, waiting for transfers between devices, per_device(): whole_rows = lax.all_gather(hidden_in, 'tp', axis=1, tiled=True)  70.7 us
    while x64, local copies, waits for them, and re-layouts  41 us
    another operation x1, loops' own time, per_device(): lax.fori_loop(0, reach, relay_step, (pair_block, own_marks, carry_state))[2]  40.4 us
    ppermute x66, waiting for transfers between devices, passed_along(): lax.ppermute(value, axis, [(source, source + steps) for source in range(f...  24.8 us
    slice x32, local copies, waits for them, and re-layouts, visit_block(): tail_mark = key_marks[key_marks.shape[0] - 1]  20.7 us
    slice x32, local copies, waits for them, and re-layouts, visit_block(): relevant = tail_mark == query_marks[0]  16.2 us
  transfers between devices with their start and end apart: 68, of which 36 were waited for; matrix products, arithmetic and copies ran while one was open for 10% of the time, Pallas kernels for 0%

commit v1 on v0

--- a/solution.py
+++ b/solution.py
@@ -82,7 +82,15 @@
     local_heads = w_out.shape[0] // HD
     my_index = lax.axis_index("ctx")
     reach = lax.axis_size("ctx") // 2
-    whole_rows = lax.all_gather(hidden_in, "tp", axis=1, tiled=True)
+    whole_rows = jnp.concatenate(
+        lax.all_to_all(
+            jnp.stack([hidden_in for _ in range(lax.psum(1, axis_name="tp"))]),
+            axis_name="tp",
+            split_axis=0,
+            concat_axis=0,
+        ),
+        axis=1,
+    )
     normed = normalize(whole_rows.astype(jnp.float32), ln_gain, ln_bias).astype(jnp.bfloat16)
     projected = jnp.einsum("td,jdh->tjh", normed, w_qkv, preferred_element_type=jnp.float32)
     starts = jnp.cumsum(prompt_lengths) - prompt_lengths

time: 720 us -> 696 us (0.967)
  waiting for transfers between devices: 239 us -> 191 us
  starting transfers between devices: 307 us -> 325 us
    all_gather x1 -> x0, waiting for transfers between devices: 70.7 us -> none  [per_device(): whole_rows = lax.all_gather(hidden_in, 'tp', axis=1, tiled=True)]
    all_to_all x0 -> x1, waiting for transfers between devices: none -> 27.3 us  [per_device(): lax.all_to_all(jnp.stack([hidden_in for _ in range(lax.psum(1, axis_name=...]
    all_to_all x0 -> x1, starting transfers between devices: none -> 12.7 us  [per_device(): lax.all_to_all(jnp.stack([hidden_in for _ in range(lax.psum(1, axis_name=...]
where the time goes in v1:
time: 696 us; the launch traced here: 692 us
  starting transfers between devices  325 us (47%)
  waiting for transfers between devices  191 us (27%)
  local copies, waits for them, and re-layouts  94.8 us (14%)
  loops' own time  43.2 us (6%)
  matrix products  14.8 us (2%)
  between operations  14.2 us (2%)
  other arithmetic  9.35 us (1%)
    ppermute x66, starting transfers between devices, passed_along(): lax.ppermute(value, axis, [(source, source + steps) for source in range(f...  312 us
    reduce_scatter x1, waiting for transfers between devices, per_device(): lax.psum_scatter(partial_value.astype(jnp.bfloat16), 'tp', scatter_dimens...  145 us
    another operation x1, loops' own time, per_device(): lax.fori_loop(0, reach, relay_step, (pair_block, own_marks, carry_state))[2]  43.1 us
    while x64, local copies, waits for them, and re-layouts  40.9 us
    all_to_all x1, waiting for transfers between devices, per_device(): lax.all_to_all(jnp.stack([hidden_in for _ in range(lax.psum(1, axis_name=...  27.3 us
    slice x32, local copies, waits for them, and re-layouts, visit_block(): tail_mark = key_marks[key_marks.shape[0] - 1]  18.6 us
    slice x32, local copies, waits for them, and re-layouts, visit_block(): relevant = tail_mark == query_marks[0]  18.5 us
    ppermute x66, waiting for transfers between devices, passed_along(): lax.ppermute(value, axis, [(source, source + steps) for source in range(f...  18.5 us
  transfers between devices with their start and end apart: 68, of which 36 were waited for; matrix products, arithmetic and copies ran while one was open for 10% of the time, Pallas kernels for 0%

profile of v1, /device:TPU:8, one launch (start us, length us, event | category | flops | bytes accessed | tf_op | source)
XLA Modules:
  0.0 691.6 jit_solution(15824494934861926205)
XLA Ops:
  9.4 12.7 %all-to-all-start = ((bf16[8,256,256]{2,1,0:T(8,128)(2,1)}), bf16[8,256,256]{2,1,0:T(8,128)(2,1)}, u32[]{:S(2)}, u32[]{:S(2)}) async-start(bf16[8,256,256]{2,1,0:T(8,128)(2,1)} %stack.6), calls=%async_computation | async-start | bytes 2097152 | tf_op jit(solution)/shard_map/all_to_all | solution.py:86
  23.7 27.3 %all-to-all-done = bf16[8,256,256]{2,1,0:T(8,128)(2,1)} async-done(((bf16[8,256,256]{2,1,0:T(8,128)(2,1)}), bf16[8,256,256]{2,1,0:T(8,128)(2,1)}, u32[]{:S(2)}, u32[]{:S(2)}) %all-to-all-start) | async-done | bytes 1048608 | tf_op jit(solution)/shard_map/all_to_all | solution.py:86
  68.0 447.9 %while.18 = (s32[]{:T(128)}, bf16[256,2,1,256]{3,0,2,1:T(8,128)(2,1)}, s32[256]{0:T(256)}, f32[1,256]{1,0:T(1,128)S(1)}, f32[1,256]{1,0:T(1,128)S(1)}, /*index=5...) while((s32[]{:T(128)}, bf16[256,2,1,256]{3,0,2,1:T(8,128)(2,1)}, ...), condition=%wide.region_11.12_spmd, body=%wide.region_6.11_spmd.sunk | while | flops 67764736 | bytes 3431739 | solution.py:121
  69.9 3.6 collective-permute-start.1
  78.4 3.2 conditional.2
  84.3 3.6 collective-permute-start.1
  92.8 3.2 conditional.2
  98.6 3.6 collective-permute-start.1
  107.8 4.4 collective-permute-start
  112.2 4.3 collective-permute-start.1
  123.4 8.0 %collective-permute-start.1 = (s32[256]{0:T(256)}, s32[256]{0:T(256)S(1)}, u32[]{:S(2)}, u32[]{:S(2)}) collective-permute-start(s32[256]{0:T(256)} %get-tuple-element.222), channel_id=1, source_target_pairs={{0,8},{8,16},{16,24},{24,32},{32,40},{40,48},{48,56},{56,64},{64,7... | collective-permute-start | bytes 3080 | tf_op jit(solution)/shard_map/while/body/eval_jaxpr/ppermute | solution.py:15
  135.4 2.9 collective-permute-start
  138.3 5.4 collective-permute-start.1
  147.8 6.1 collective-permute-start
  153.9 5.4 collective-permute-start.1
  163.4 2.9 collective-permute-start
  166.2 8.6 %collective-permute-start.1 = (s32[256]{0:T(256)}, s32[256]{0:T(256)S(1)}, u32[]{:S(2)}, u32[]{:S(2)}) collective-permute-start(s32[256]{0:T(256)} %get-tuple-element.222), channel_id=1, source_target_pairs={{0,8},{8,16},{16,24},{24,32},{32,40},{40,48},{48,56},{56,64},{64,7... | collective-permute-start | bytes 3080 | tf_op jit(solution)/shard_map/while/body/eval_jaxpr/ppermute | solution.py:15
  181.8 5.4 collective-permute-start.1
  191.3 6.1 collective-permute-start
  197.4 5.4 collective-permute-start.1
  206.8 2.9 collective-permute-start
  209.7 8.6 %collective-permute-start.1 = (s32[256]{0:T(256)}, s32[256]{0:T(256)S(1)}, u32[]{:S(2)}, u32[]{:S(2)}) collective-permute-start(s32[256]{0:T(256)} %get-tuple-element.222), channel_id=1, source_target_pairs={{0,8},{8,16},{16,24},{24,32},{32,40},{40,48},{48,56},{56,64},{64,7... | collective-permute-start | bytes 3080 | tf_op jit(solution)/shard_map/while/body/eval_jaxpr/ppermute | solution.py:15
  225.3 5.4 collective-permute-start.1
  237.6 5.4 collective-permute-start.1
  250.0 5.4 collective-permute-start.1
  262.3 5.4 collective-permute-start.1
  271.8 5.9 collective-permute-start
  277.7 6.1 collective-permute-start.1
  287.8 3.1 collective-permute-start
  290.9 9.3 %collective-permute-start.1 = (s32[256]{0:T(256)}, s32[256]{0:T(256)S(1)}, u32[]{:S(2)}, u32[]{:S(2)}) collective-permute-start(s32[256]{0:T(256)} %get-tuple-element.222), channel_id=1, source_target_pairs={{0,8},{8,16},{16,24},{24,32},{32,40},{40,48},{48,56},{56,64},{64,7... | collective-permute-start | bytes 3080 | tf_op jit(solution)/shard_map/while/body/eval_jaxpr/ppermute | solution.py:15
  304.3 3.1 collective-permute-start
  307.4 6.1 collective-permute-start.1
  317.5 6.3 collective-permute-start
  323.9 6.1 collective-permute-start.1
  334.0 3.1 collective-permute-start
  337.1 9.3 %collective-permute-start.1 = (s32[256]{0:T(256)}, s32[256]{0:T(256)S(1)}, u32[]{:S(2)}, u32[]{:S(2)}) collective-permute-start(s32[256]{0:T(256)} %get-tuple-element.222), channel_id=1, source_target_pairs={{0,8},{8,16},{16,24},{24,32},{32,40},{40,48},{48,56},{56,64},{64,7... | collective-permute-start | bytes 3080 | tf_op jit(solution)/shard_map/while/body/eval_jaxpr/ppermute | solution.py:15
  350.5 3.1 collective-permute-start
  353.6 6.1 collective-permute-start.1
  363.7 6.3 collective-permute-start
  370.0 6.1 collective-permute-start.1
  380.2 3.1 collective-permute-start
  383.3 9.3 %collective-permute-start.1 = (s32[256]{0:T(256)}, s32[256]{0:T(256)S(1)}, u32[]{:S(2)}, u32[]{:S(2)}) collective-permute-start(s32[256]{0:T(256)} %get-tuple-element.222), channel_id=1, source_target_pairs={{0,8},{8,16},{16,24},{24,32},{32,40},{40,48},{48,56},{56,64},{64,7... | collective-permute-start | bytes 3080 | tf_op jit(solution)/shard_map/while/body/eval_jaxpr/ppermute | solution.py:15
  396.6 3.1 collective-permute-start
  399.7 6.1 collective-permute-start.1
  409.9 3.1 collective-permute-start
  413.0 6.1 collective-permute-start.1
  423.1 3.1 collective-permute-start
  426.2 6.1 collective-permute-start.1
  436.4 3.1 collective-permute-start
  439.5 6.1 collective-permute-start.1
  449.6 3.1 collective-permute-start
  452.7 6.1 collective-permute-start.1
  462.9 3.1 collective-permute-start
  466.0 6.1 collective-permute-start.1
  476.1 3.1 collective-permute-start
  479.2 6.1 collective-permute-start.1
  489.4 3.1 collective-permute-start
  492.5 6.1 collective-permute-start.1
  502.6 3.1 collective-permute-start
  505.7 6.1 collective-permute-start.1
  523.3 3.9 gather_fusion
  527.3 3.1 collective-permute-start.3
  531.1 3.7 collective-permute-done.3
  539.8 144.9 %reduce-scatter.2.cloned.1.call-done = bf16[256,256]{1,0:T(8,128)(2,1)} async-done(((bf16[256,2048]{1,0:T(8,128)(2,1)}), bf16[256,256]{1,0:T(8,128)(2,1)}) %reduce-scatter.2.cloned.1.call-update) | async-done | bytes 131088 | tf_op jit(solution)/shard_map/reduce_scatter | solution.py:130
  (317 shorter events, 154.6 us)
Async XLA Ops:
  9.4 41.6 %all-to-all-start = ((bf16[8,256,256]{2,1,0:T(8,128)(2,1)}), bf16[8,256,256]{2,1,0:T(8,128)(2,1)}, u32[]{:S(2)}, u32[]{:S(2)}) async-start(bf16[8,256,256]{2,1,0:T(8,128)(2,1)} %stack.6), calls=%async_computation | async-start | bytes 2097152 | tf_op jit(solution)/shard_map/all_to_all | solution.py:86
  22.1 662.6 %reduce-scatter.2.cloned.1.call-start = ((), (), s32[]{:S(2)}) async-start(), calls=%async_computation.2 | async-start | bytes 1179648 | tf_op jit(solution)/shard_map/reduce_scatter | solution.py:130
  68.0 10.4 %collective-permute-start = (bf16[256,2,1,256]{3,0,2,1:T(8,128)(2,1)}, bf16[256,2,1,256]{3,0,2,1:T(8,128)(2,1)S(1)}, u32[]{:S(2)}, u32[]{:S(2)}) collective-permute-start(bf16[256,2,1,256]{3,0,2,1:T(8,128)(2,1)} %get-tuple-element.221), channel_id=1, source_target_pairs={{0,8},{8,16},{16,24},{24,32},{32,40},{40,48},{48,56},{56,64},{64,7... | collective-permute-start | bytes 786440 | tf_op jit(solution)/shard_map/while/body/eval_jaxpr/ppermute | solution.py:15
  69.9 6.0 collective-permute-start.1
  82.3 10.4 %collective-permute-start = (bf16[256,2,1,256]{3,0,2,1:T(8,128)(2,1)}, bf16[256,2,1,256]{3,0,2,1:T(8,128)(2,1)S(1)}, u32[]{:S(2)}, u32[]{:S(2)}) collective-permute-start(bf16[256,2,1,256]{3,0,2,1:T(8,128)(2,1)} %get-tuple-element.221), channel_id=1, source_target_pairs={{0,8},{8,16},{16,24},{24,32},{32,40},{40,48},{48,56},{56,64},{64,7... | collective-permute-start | bytes 786440 | tf_op jit(solution)/shard_map/while/body/eval_jaxpr/ppermute | solution.py:15
  96.7 10.4 %collective-permute-start = (bf16[256,2,1,256]{3,0,2,1:T(8,128)(2,1)}, bf16[256,2,1,256]{3,0,2,1:T(8,128)(2,1)S(1)}, u32[]{:S(2)}, u32[]{:S(2)}) collective-permute-start(bf16[256,2,1,256]{3,0,2,1:T(8,128)(2,1)} %get-tuple-element.221), channel_id=1, source_target_pairs={{0,8},{8,16},{16,24},{24,32},{32,40},{40,48},{48,56},{56,64},{64,7... | collective-permute-start | bytes 786440 | tf_op jit(solution)/shard_map/while/body/eval_jaxpr/ppermute | solution.py:15
  107.8 12.1 %collective-permute-start = (bf16[256,2,1,256]{3,0,2,1:T(8,128)(2,1)}, bf16[256,2,1,256]{3,0,2,1:T(8,128)(2,1)S(1)}, u32[]{:S(2)}, u32[]{:S(2)}) collective-permute-start(bf16[256,2,1,256]{3,0,2,1:T(8,128)(2,1)} %get-tuple-element.221), channel_id=1, source_target_pairs={{0,8},{8,16},{16,24},{24,32},{32,40},{40,48},{48,56},{56,64},{64,7... | collective-permute-start | bytes 786440 | tf_op jit(solution)/shard_map/while/body/eval_jaxpr/ppermute | solution.py:15
  120.6 14.1 %collective-permute-start = (bf16[256,2,1,256]{3,0,2,1:T(8,128)(2,1)}, bf16[256,2,1,256]{3,0,2,1:T(8,128)(2,1)S(1)}, u32[]{:S(2)}, u32[]{:S(2)}) collective-permute-start(bf16[256,2,1,256]{3,0,2,1:T(8,128)(2,1)} %get-tuple-element.221), channel_id=1, source_target_pairs={{0,8},{8,16},{16,24},{24,32},{32,40},{40,48},{48,56},{56,64},{64,7... | collective-permute-start | bytes 786440 | tf_op jit(solution)/shard_map/while/body/eval_jaxpr/ppermute | solution.py:15
  123.4 8.9 %collective-permute-start.1 = (s32[256]{0:T(256)}, s32[256]{0:T(256)S(1)}, u32[]{:S(2)}, u32[]{:S(2)}) collective-permute-start(s32[256]{0:T(256)} %get-tuple-element.222), channel_id=1, source_target_pairs={{0,8},{8,16},{16,24},{24,32},{32,40},{40,48},{48,56},{56,64},{64,7... | collective-permute-start | bytes 3080 | tf_op jit(solution)/shard_map/while/body/eval_jaxpr/ppermute | solution.py:15
  135.4 11.6 %collective-permute-start = (bf16[256,2,1,256]{3,0,2,1:T(8,128)(2,1)}, bf16[256,2,1,256]{3,0,2,1:T(8,128)(2,1)S(1)}, u32[]{:S(2)}, u32[]{:S(2)}) collective-permute-start(bf16[256,2,1,256]{3,0,2,1:T(8,128)(2,1)} %get-tuple-element.221), channel_id=1, source_target_pairs={{0,8},{8,16},{16,24},{24,32},{32,40},{40,48},{48,56},{56,64},{64,7... | collective-permute-start | bytes 786440 | tf_op jit(solution)/shard_map/while/body/eval_jaxpr/ppermute | solution.py:15
  138.3 6.3 collective-permute-start.1
  147.8 14.9 %collective-permute-start = (bf16[256,2,1,256]{3,0,2,1:T(8,128)(2,1)}, bf16[256,2,1,256]{3,0,2,1:T(8,128)(2,1)S(1)}, u32[]{:S(2)}, u32[]{:S(2)}) collective-permute-start(bf16[256,2,1,256]{3,0,2,1:T(8,128)(2,1)} %get-tuple-element.221), channel_id=1, source_target_pairs={{0,8},{8,16},{16,24},{24,32},{32,40},{40,48},{48,56},{56,64},{64,7... | collective-permute-start | bytes 786440 | tf_op jit(solution)/shard_map/while/body/eval_jaxpr/ppermute | solution.py:15
  153.9 6.3 collective-permute-start.1
  163.4 14.9 %collective-permute-start = (bf16[256,2,1,256]{3,0,2,1:T(8,128)(2,1)}, bf16[256,2,1,256]{3,0,2,1:T(8,128)(2,1)S(1)}, u32[]{:S(2)}, u32[]{:S(2)}) collective-permute-start(bf16[256,2,1,256]{3,0,2,1:T(8,128)(2,1)} %get-tuple-element.221), channel_id=1, source_target_pairs={{0,8},{8,16},{16,24},{24,32},{32,40},{40,48},{48,56},{56,64},{64,7... | collective-permute-start | bytes 786440 | tf_op jit(solution)/shard_map/while/body/eval_jaxpr/ppermute | solution.py:15
  166.2 9.5 %collective-permute-start.1 = (s32[256]{0:T(256)}, s32[256]{0:T(256)S(1)}, u32[]{:S(2)}, u32[]{:S(2)}) collective-permute-start(s32[256]{0:T(256)} %get-tuple-element.222), channel_id=1, source_target_pairs={{0,8},{8,16},{16,24},{24,32},{32,40},{40,48},{48,56},{56,64},{64,7... | collective-permute-start | bytes 3080 | tf_op jit(solution)/shard_map/while/body/eval_jaxpr/ppermute | solution.py:15
  178.9 11.6 %collective-permute-start = (bf16[256,2,1,256]{3,0,2,1:T(8,128)(2,1)}, bf16[256,2,1,256]{3,0,2,1:T(8,128)(2,1)S(1)}, u32[]{:S(2)}, u32[]{:S(2)}) collective-permute-start(bf16[256,2,1,256]{3,0,2,1:T(8,128)(2,1)} %get-tuple-element.221), channel_id=1, source_target_pairs={{0,8},{8,16},{16,24},{24,32},{32,40},{40,48},{48,56},{56,64},{64,7... | collective-permute-start | bytes 786440 | tf_op jit(solution)/shard_map/while/body/eval_jaxpr/ppermute | solution.py:15
  181.8 6.3 collective-permute-start.1
  191.3 14.9 %collective-permute-start = (bf16[256,2,1,256]{3,0,2,1:T(8,128)(2,1)}, bf16[256,2,1,256]{3,0,2,1:T(8,128)(2,1)S(1)}, u32[]{:S(2)}, u32[]{:S(2)}) collective-permute-start(bf16[256,2,1,256]{3,0,2,1:T(8,128)(2,1)} %get-tuple-element.221), channel_id=1, source_target_pairs={{0,8},{8,16},{16,24},{24,32},{32,40},{40,48},{48,56},{56,64},{64,7... | collective-permute-start | bytes 786440 | tf_op jit(solution)/shard_map/while/body/eval_jaxpr/ppermute | solution.py:15
  197.4 6.3 collective-permute-start.1
  206.8 14.9 %collective-permute-start = (bf16[256,2,1,256]{3,0,2,1:T(8,128)(2,1)}, bf16[256,2,1,256]{3,0,2,1:T(8,128)(2,1)S(1)}, u32[]{:S(2)}, u32[]{:S(2)}) collective-permute-start(bf16[256,2,1,256]{3,0,2,1:T(8,128)(2,1)} %get-tuple-element.221), channel_id=1, source_target_pairs={{0,8},{8,16},{16,24},{24,32},{32,40},{40,48},{48,56},{56,64},{64,7... | collective-permute-start | bytes 786440 | tf_op jit(solution)/shard_map/while/body/eval_jaxpr/ppermute | solution.py:15
  209.7 9.5 %collective-permute-start.1 = (s32[256]{0:T(256)}, s32[256]{0:T(256)S(1)}, u32[]{:S(2)}, u32[]{:S(2)}) collective-permute-start(s32[256]{0:T(256)} %get-tuple-element.222), channel_id=1, source_target_pairs={{0,8},{8,16},{16,24},{24,32},{32,40},{40,48},{48,56},{56,64},{64,7... | collective-permute-start | bytes 3080 | tf_op jit(solution)/shard_map/while/body/eval_jaxpr/ppermute | solution.py:15
  222.4 11.6 %collective-permute-start = (bf16[256,2,1,256]{3,0,2,1:T(8,128)(2,1)}, bf16[256,2,1,256]{3,0,2,1:T(8,128)(2,1)S(1)}, u32[]{:S(2)}, u32[]{:S(2)}) collective-permute-start(bf16[256,2,1,256]{3,0,2,1:T(8,128)(2,1)} %get-tuple-element.221), channel_id=1, source_target_pairs={{0,8},{8,16},{16,24},{24,32},{32,40},{40,48},{48,56},{56,64},{64,7... | collective-permute-start | bytes 786440 | tf_op jit(solution)/shard_map/while/body/eval_jaxpr/ppermute | solution.py:15
  225.3 6.3 collective-permute-start.1
  234.8 11.6 %collective-permute-start = (bf16[256,2,1,256]{3,0,2,1:T(8,128)(2,1)}, bf16[256,2,1,256]{3,0,2,1:T(8,128)(2,1)S(1)}, u32[]{:S(2)}, u32[]{:S(2)}) collective-permute-start(bf16[256,2,1,256]{3,0,2,1:T(8,128)(2,1)} %get-tuple-element.221), channel_id=1, source_target_pairs={{0,8},{8,16},{16,24},{24,32},{32,40},{40,48},{48,56},{56,64},{64,7... | collective-permute-start | bytes 786440 | tf_op jit(solution)/shard_map/while/body/eval_jaxpr/ppermute | solution.py:15
  237.6 6.3 collective-permute-start.1
  247.1 11.6 %collective-permute-start = (bf16[256,2,1,256]{3,0,2,1:T(8,128)(2,1)}, bf16[256,2,1,256]{3,0,2,1:T(8,128)(2,1)S(1)}, u32[]{:S(2)}, u32[]{:S(2)}) collective-permute-start(bf16[256,2,1,256]{3,0,2,1:T(8,128)(2,1)} %get-tuple-element.221), channel_id=1, source_target_pairs={{0,8},{8,16},{16,24},{24,32},{32,40},{40,48},{48,56},{56,64},{64,7... | collective-permute-start | bytes 786440 | tf_op jit(solution)/shard_map/while/body/eval_jaxpr/ppermute | solution.py:15
  250.0 6.3 collective-permute-start.1
  259.5 11.6 %collective-permute-start = (bf16[256,2,1,256]{3,0,2,1:T(8,128)(2,1)}, bf16[256,2,1,256]{3,0,2,1:T(8,128)(2,1)S(1)}, u32[]{:S(2)}, u32[]{:S(2)}) collective-permute-start(bf16[256,2,1,256]{3,0,2,1:T(8,128)(2,1)} %get-tuple-element.221), channel_id=1, source_target_pairs={{0,8},{8,16},{16,24},{24,32},{32,40},{40,48},{48,56},{56,64},{64,7... | collective-permute-start | bytes 786440 | tf_op jit(solution)/shard_map/while/body/eval_jaxpr/ppermute | solution.py:15
  262.3 6.3 collective-permute-start.1
  271.8 15.3 %collective-permute-start = (bf16[256,2,1,256]{3,0,2,1:T(8,128)(2,1)}, bf16[256,2,1,256]{3,0,2,1:T(8,128)(2,1)S(1)}, u32[]{:S(2)}, u32[]{:S(2)}) collective-permute-start(bf16[256,2,1,256]{3,0,2,1:T(8,128)(2,1)} %get-tuple-element.221), channel_id=1, source_target_pairs={{0,8},{8,16},{16,24},{24,32},{32,40},{40,48},{48,56},{56,64},{64,7... | collective-permute-start | bytes 786440 | tf_op jit(solution)/shard_map/while/body/eval_jaxpr/ppermute | solution.py:15
  277.7 7.0 %collective-permute-start.1 = (s32[256]{0:T(256)}, s32[256]{0:T(256)S(1)}, u32[]{:S(2)}, u32[]{:S(2)}) collective-permute-start(s32[256]{0:T(256)} %get-tuple-element.222), channel_id=1, source_target_pairs={{0,8},{8,16},{16,24},{24,32},{32,40},{40,48},{48,56},{56,64},{64,7... | collective-permute-start | bytes 3080 | tf_op jit(solution)/shard_map/while/body/eval_jaxpr/ppermute | solution.py:15
  287.8 15.8 %collective-permute-start = (bf16[256,2,1,256]{3,0,2,1:T(8,128)(2,1)}, bf16[256,2,1,256]{3,0,2,1:T(8,128)(2,1)S(1)}, u32[]{:S(2)}, u32[]{:S(2)}) collective-permute-start(bf16[256,2,1,256]{3,0,2,1:T(8,128)(2,1)} %get-tuple-element.221), channel_id=1, source_target_pairs={{0,8},{8,16},{16,24},{24,32},{32,40},{40,48},{48,56},{56,64},{64,7... | collective-permute-start | bytes 786440 | tf_op jit(solution)/shard_map/while/body/eval_jaxpr/ppermute | solution.py:15
  290.9 10.2 %collective-permute-start.1 = (s32[256]{0:T(256)}, s32[256]{0:T(256)S(1)}, u32[]{:S(2)}, u32[]{:S(2)}) collective-permute-start(s32[256]{0:T(256)} %get-tuple-element.222), channel_id=1, source_target_pairs={{0,8},{8,16},{16,24},{24,32},{32,40},{40,48},{48,56},{56,64},{64,7... | collective-permute-start | bytes 3080 | tf_op jit(solution)/shard_map/while/body/eval_jaxpr/ppermute | solution.py:15
  304.3 12.5 %collective-permute-start = (bf16[256,2,1,256]{3,0,2,1:T(8,128)(2,1)}, bf16[256,2,1,256]{3,0,2,1:T(8,128)(2,1)S(1)}, u32[]{:S(2)}, u32[]{:S(2)}) collective-permute-start(bf16[256,2,1,256]{3,0,2,1:T(8,128)(2,1)} %get-tuple-element.221), channel_id=1, source_target_pairs={{0,8},{8,16},{16,24},{24,32},{32,40},{40,48},{48,56},{56,64},{64,7... | collective-permute-start | bytes 786440 | tf_op jit(solution)/shard_map/while/body/eval_jaxpr/ppermute | solution.py:15
  307.4 7.0 %collective-permute-start.1 = (s32[256]{0:T(256)}, s32[256]{0:T(256)S(1)}, u32[]{:S(2)}, u32[]{:S(2)}) collective-permute-start(s32[256]{0:T(256)} %get-tuple-element.222), channel_id=1, source_target_pairs={{0,8},{8,16},{16,24},{24,32},{32,40},{40,48},{48,56},{56,64},{64,7... | collective-permute-start | bytes 3080 | tf_op jit(solution)/shard_map/while/body/eval_jaxpr/ppermute | solution.py:15
  317.5 15.8 %collective-permute-start = (bf16[256,2,1,256]{3,0,2,1:T(8,128)(2,1)}, bf16[256,2,1,256]{3,0,2,1:T(8,128)(2,1)S(1)}, u32[]{:S(2)}, u32[]{:S(2)}) collective-permute-start(bf16[256,2,1,256]{3,0,2,1:T(8,128)(2,1)} %get-tuple-element.221), channel_id=1, source_target_pairs={{0,8},{8,16},{16,24},{24,32},{32,40},{40,48},{48,56},{56,64},{64,7... | collective-permute-start | bytes 786440 | tf_op jit(solution)/shard_map/while/body/eval_jaxpr/ppermute | solution.py:15
  323.9 7.0 %collective-permute-start.1 = (s32[256]{0:T(256)}, s32[256]{0:T(256)S(1)}, u32[]{:S(2)}, u32[]{:S(2)}) collective-permute-start(s32[256]{0:T(256)} %get-tuple-element.222), channel_id=1, source_target_pairs={{0,8},{8,16},{16,24},{24,32},{32,40},{40,48},{48,56},{56,64},{64,7... | collective-permute-start | bytes 3080 | tf_op jit(solution)/shard_map/while/body/eval_jaxpr/ppermute | solution.py:15
  334.0 15.8 %collective-permute-start = (bf16[256,2,1,256]{3,0,2,1:T(8,128)(2,1)}, bf16[256,2,1,256]{3,0,2,1:T(8,128)(2,1)S(1)}, u32[]{:S(2)}, u32[]{:S(2)}) collective-permute-start(bf16[256,2,1,256]{3,0,2,1:T(8,128)(2,1)} %get-tuple-element.221), channel_id=1, source_target_pairs={{0,8},{8,16},{16,24},{24,32},{32,40},{40,48},{48,56},{56,64},{64,7... | collective-permute-start | bytes 786440 | tf_op jit(solution)/shard_map/while/body/eval_jaxpr/ppermute | solution.py:15
  337.1 10.2 %collective-permute-start.1 = (s32[256]{0:T(256)}, s32[256]{0:T(256)S(1)}, u32[]{:S(2)}, u32[]{:S(2)}) collective-permute-start(s32[256]{0:T(256)} %get-tuple-element.222), channel_id=1, source_target_pairs={{0,8},{8,16},{16,24},{24,32},{32,40},{40,48},{48,56},{56,64},{64,7... | collective-permute-start | bytes 3080 | tf_op jit(solution)/shard_map/while/body/eval_jaxpr/ppermute | solution.py:15
  350.5 12.5 %collective-permute-start = (bf16[256,2,1,256]{3,0,2,1:T(8,128)(2,1)}, bf16[256,2,1,256]{3,0,2,1:T(8,128)(2,1)S(1)}, u32[]{:S(2)}, u32[]{:S(2)}) collective-permute-start(bf16[256,2,1,256]{3,0,2,1:T(8,128)(2,1)} %get-tuple-element.221), channel_id=1, source_target_pairs={{0,8},{8,16},{16,24},{24,32},{32,40},{40,48},{48,56},{56,64},{64,7... | collective-permute-start | bytes 786440 | tf_op jit(solution)/shard_map/while/body/eval_jaxpr/ppermute | solution.py:15
  353.6 7.0 %collective-permute-start.1 = (s32[256]{0:T(256)}, s32[256]{0:T(256)S(1)}, u32[]{:S(2)}, u32[]{:S(2)}) collective-permute-start(s32[256]{0:T(256)} %get-tuple-element.222), channel_id=1, source_target_pairs={{0,8},{8,16},{16,24},{24,32},{32,40},{40,48},{48,56},{56,64},{64,7... | collective-permute-start | bytes 3080 | tf_op jit(solution)/shard_map/while/body/eval_jaxpr/ppermute | solution.py:15
  363.7 15.8 %collective-permute-start = (bf16[256,2,1,256]{3,0,2,1:T(8,128)(2,1)}, bf16[256,2,1,256]{3,0,2,1:T(8,128)(2,1)S(1)}, u32[]{:S(2)}, u32[]{:S(2)}) collective-permute-start(bf16[256,2,1,256]{3,0,2,1:T(8,128)(2,1)} %get-tuple-element.221), channel_id=1, source_target_pairs={{0,8},{8,16},{16,24},{24,32},{32,40},{40,48},{48,56},{56,64},{64,7... | collective-permute-start | bytes 786440 | tf_op jit(solution)/shard_map/while/body/eval_jaxpr/ppermute | solution.py:15
  370.0 7.0 %collective-permute-start.1 = (s32[256]{0:T(256)}, s32[256]{0:T(256)S(1)}, u32[]{:S(2)}, u32[]{:S(2)}) collective-permute-start(s32[256]{0:T(256)} %get-tuple-element.222), channel_id=1, source_target_pairs={{0,8},{8,16},{16,24},{24,32},{32,40},{40,48},{48,56},{56,64},{64,7... | collective-permute-start | bytes 3080 | tf_op jit(solution)/shard_map/while/body/eval_jaxpr/ppermute | solution.py:15
  380.2 15.8 %collective-permute-start = (bf16[256,2,1,256]{3,0,2,1:T(8,128)(2,1)}, bf16[256,2,1,256]{3,0,2,1:T(8,128)(2,1)S(1)}, u32[]{:S(2)}, u32[]{:S(2)}) collective-permute-start(bf16[256,2,1,256]{3,0,2,1:T(8,128)(2,1)} %get-tuple-element.221), channel_id=1, source_target_pairs={{0,8},{8,16},{16,24},{24,32},{32,40},{40,48},{48,56},{56,64},{64,7... | collective-permute-start | bytes 786440 | tf_op jit(solution)/shard_map/while/body/eval_jaxpr/ppermute | solution.py:15
  383.3 10.2 %collective-permute-start.1 = (s32[256]{0:T(256)}, s32[256]{0:T(256)S(1)}, u32[]{:S(2)}, u32[]{:S(2)}) collective-permute-start(s32[256]{0:T(256)} %get-tuple-element.222), channel_id=1, source_target_pairs={{0,8},{8,16},{16,24},{24,32},{32,40},{40,48},{48,56},{56,64},{64,7... | collective-permute-start | bytes 3080 | tf_op jit(solution)/shard_map/while/body/eval_jaxpr/ppermute | solution.py:15
  396.6 12.5 %collective-permute-start = (bf16[256,2,1,256]{3,0,2,1:T(8,128)(2,1)}, bf16[256,2,1,256]{3,0,2,1:T(8,128)(2,1)S(1)}, u32[]{:S(2)}, u32[]{:S(2)}) collective-permute-start(bf16[256,2,1,256]{3,0,2,1:T(8,128)(2,1)} %get-tuple-element.221), channel_id=1, source_target_pairs={{0,8},{8,16},{16,24},{24,32},{32,40},{40,48},{48,56},{56,64},{64,7... | collective-permute-start | bytes 786440 | tf_op jit(solution)/shard_map/while/body/eval_jaxpr/ppermute | solution.py:15
  399.7 7.0 %collective-permute-start.1 = (s32[256]{0:T(256)}, s32[256]{0:T(256)S(1)}, u32[]{:S(2)}, u32[]{:S(2)}) collective-permute-start(s32[256]{0:T(256)} %get-tuple-element.222), channel_id=1, source_target_pairs={{0,8},{8,16},{16,24},{24,32},{32,40},{40,48},{48,56},{56,64},{64,7... | collective-permute-start | bytes 3080 | tf_op jit(solution)/shard_map/while/body/eval_jaxpr/ppermute | solution.py:15
  409.9 12.5 %collective-permute-start = (bf16[256,2,1,256]{3,0,2,1:T(8,128)(2,1)}, bf16[256,2,1,256]{3,0,2,1:T(8,128)(2,1)S(1)}, u32[]{:S(2)}, u32[]{:S(2)}) collective-permute-start(bf16[256,2,1,256]{3,0,2,1:T(8,128)(2,1)} %get-tuple-element.221), channel_id=1, source_target_pairs={{0,8},{8,16},{16,24},{24,32},{32,40},{40,48},{48,56},{56,64},{64,7... | collective-permute-start | bytes 786440 | tf_op jit(solution)/shard_map/while/body/eval_jaxpr/ppermute | solution.py:15
  413.0 7.0 %collective-permute-start.1 = (s32[256]{0:T(256)}, s32[256]{0:T(256)S(1)}, u32[]{:S(2)}, u32[]{:S(2)}) collective-permute-start(s32[256]{0:T(256)} %get-tuple-element.222), channel_id=1, source_target_pairs={{0,8},{8,16},{16,24},{24,32},{32,40},{40,48},{48,56},{56,64},{64,7... | collective-permute-start | bytes 3080 | tf_op jit(solution)/shard_map/while/body/eval_jaxpr/ppermute | solution.py:15
  423.1 12.5 %collective-permute-start = (bf16[256,2,1,256]{3,0,2,1:T(8,128)(2,1)}, bf16[256,2,1,256]{3,0,2,1:T(8,128)(2,1)S(1)}, u32[]{:S(2)}, u32[]{:S(2)}) collective-permute-start(bf16[256,2,1,256]{3,0,2,1:T(8,128)(2,1)} %get-tuple-element.221), channel_id=1, source_target_pairs={{0,8},{8,16},{16,24},{24,32},{32,40},{40,48},{48,56},{56,64},{64,7... | collective-permute-start | bytes 786440 | tf_op jit(solution)/shard_map/while/body/eval_jaxpr/ppermute | solution.py:15
  426.2 7.0 %collective-permute-start.1 = (s32[256]{0:T(256)}, s32[256]{0:T(256)S(1)}, u32[]{:S(2)}, u32[]{:S(2)}) collective-permute-start(s32[256]{0:T(256)} %get-tuple-element.222), channel_id=1, source_target_pairs={{0,8},{8,16},{16,24},{24,32},{32,40},{40,48},{48,56},{56,64},{64,7... | collective-permute-start | bytes 3080 | tf_op jit(solution)/shard_map/while/body/eval_jaxpr/ppermute | solution.py:15
  436.4 12.5 %collective-permute-start = (bf16[256,2,1,256]{3,0,2,1:T(8,128)(2,1)}, bf16[256,2,1,256]{3,0,2,1:T(8,128)(2,1)S(1)}, u32[]{:S(2)}, u32[]{:S(2)}) collective-permute-start(bf16[256,2,1,256]{3,0,2,1:T(8,128)(2,1)} %get-tuple-element.221), channel_id=1, source_target_pairs={{0,8},{8,16},{16,24},{24,32},{32,40},{40,48},{48,56},{56,64},{64,7... | collective-permute-start | bytes 786440 | tf_op jit(solution)/shard_map/while/body/eval_jaxpr/ppermute | solution.py:15
  439.5 7.0 %collective-permute-start.1 = (s32[256]{0:T(256)}, s32[256]{0:T(256)S(1)}, u32[]{:S(2)}, u32[]{:S(2)}) collective-permute-start(s32[256]{0:T(256)} %get-tuple-element.222), channel_id=1, source_target_pairs={{0,8},{8,16},{16,24},{24,32},{32,40},{40,48},{48,56},{56,64},{64,7... | collective-permute-start | bytes 3080 | tf_op jit(solution)/shard_map/while/body/eval_jaxpr/ppermute | solution.py:15
  449.6 12.5 %collective-permute-start = (bf16[256,2,1,256]{3,0,2,1:T(8,128)(2,1)}, bf16[256,2,1,256]{3,0,2,1:T(8,128)(2,1)S(1)}, u32[]{:S(2)}, u32[]{:S(2)}) collective-permute-start(bf16[256,2,1,256]{3,0,2,1:T(8,128)(2,1)} %get-tuple-element.221), channel_id=1, source_target_pairs={{0,8},{8,16},{16,24},{24,32},{32,40},{40,48},{48,56},{56,64},{64,7... | collective-permute-start | bytes 786440 | tf_op jit(solution)/shard_map/while/body/eval_jaxpr/ppermute | solution.py:15
  452.7 7.0 %collective-permute-start.1 = (s32[256]{0:T(256)}, s32[256]{0:T(256)S(1)}, u32[]{:S(2)}, u32[]{:S(2)}) collective-permute-start(s32[256]{0:T(256)} %get-tuple-element.222), channel_id=1, source_target_pairs={{0,8},{8,16},{16,24},{24,32},{32,40},{40,48},{48,56},{56,64},{64,7... | collective-permute-start | bytes 3080 | tf_op jit(solution)/shard_map/while/body/eval_jaxpr/ppermute | solution.py:15
  462.9 12.5 %collective-permute-start = (bf16[256,2,1,256]{3,0,2,1:T(8,128)(2,1)}, bf16[256,2,1,256]{3,0,2,1:T(8,128)(2,1)S(1)}, u32[]{:S(2)}, u32[]{:S(2)}) collective-permute-start(bf16[256,2,1,256]{3,0,2,1:T(8,128)(2,1)} %get-tuple-element.221), channel_id=1, source_target_pairs={{0,8},{8,16},{16,24},{24,32},{32,40},{40,48},{48,56},{56,64},{64,7... | collective-permute-start | bytes 786440 | tf_op jit(solution)/shard_map/while/body/eval_jaxpr/ppermute | solution.py:15
  466.0 7.0 %collective-permute-start.1 = (s32[256]{0:T(256)}, s32[256]{0:T(256)S(1)}, u32[]{:S(2)}, u32[]{:S(2)}) collective-permute-start(s32[256]{0:T(256)} %get-tuple-element.222), channel_id=1, source_target_pairs={{0,8},{8,16},{16,24},{24,32},{32,40},{40,48},{48,56},{56,64},{64,7... | collective-permute-start | bytes 3080 | tf_op jit(solution)/shard_map/while/body/eval_jaxpr/ppermute | solution.py:15
  476.1 12.5 %collective-permute-start = (bf16[256,2,1,256]{3,0,2,1:T(8,128)(2,1)}, bf16[256,2,1,256]{3,0,2,1:T(8,128)(2,1)S(1)}, u32[]{:S(2)}, u32[]{:S(2)}) collective-permute-start(bf16[256,2,1,256]{3,0,2,1:T(8,128)(2,1)} %get-tuple-element.221), channel_id=1, source_target_pairs={{0,8},{8,16},{16,24},{24,32},{32,40},{40,48},{48,56},{56,64},{64,7... | collective-permute-start | bytes 786440 | tf_op jit(solution)/shard_map/while/body/eval_jaxpr/ppermute | solution.py:15
  479.2 7.0 %collective-permute-start.1 = (s32[256]{0:T(256)}, s32[256]{0:T(256)S(1)}, u32[]{:S(2)}, u32[]{:S(2)}) collective-permute-start(s32[256]{0:T(256)} %get-tuple-element.222), channel_id=1, source_target_pairs={{0,8},{8,16},{16,24},{24,32},{32,40},{40,48},{48,56},{56,64},{64,7... | collective-permute-start | bytes 3080 | tf_op jit(solution)/shard_map/while/body/eval_jaxpr/ppermute | solution.py:15
  489.4 12.5 %collective-permute-start = (bf16[256,2,1,256]{3,0,2,1:T(8,128)(2,1)}, bf16[256,2,1,256]{3,0,2,1:T(8,128)(2,1)S(1)}, u32[]{:S(2)}, u32[]{:S(2)}) collective-permute-start(bf16[256,2,1,256]{3,0,2,1:T(8,128)(2,1)} %get-tuple-element.221), channel_id=1, source_target_pairs={{0,8},{8,16},{16,24},{24,32},{32,40},{40,48},{48,56},{56,64},{64,7... | collective-permute-start | bytes 786440 | tf_op jit(solution)/shard_map/while/body/eval_jaxpr/ppermute | solution.py:15
  492.5 7.0 %collective-permute-start.1 = (s32[256]{0:T(256)}, s32[256]{0:T(256)S(1)}, u32[]{:S(2)}, u32[]{:S(2)}) collective-permute-start(s32[256]{0:T(256)} %get-tuple-element.222), channel_id=1, source_target_pairs={{0,8},{8,16},{16,24},{24,32},{32,40},{40,48},{48,56},{56,64},{64,7... | collective-permute-start | bytes 3080 | tf_op jit(solution)/shard_map/while/body/eval_jaxpr/ppermute | solution.py:15
  502.6 12.5 %collective-permute-start = (bf16[256,2,1,256]{3,0,2,1:T(8,128)(2,1)}, bf16[256,2,1,256]{3,0,2,1:T(8,128)(2,1)S(1)}, u32[]{:S(2)}, u32[]{:S(2)}) collective-permute-start(bf16[256,2,1,256]{3,0,2,1:T(8,128)(2,1)} %get-tuple-element.221), channel_id=1, source_target_pairs={{0,8},{8,16},{16,24},{24,32},{32,40},{40,48},{48,56},{56,64},{64,7... | collective-permute-start | bytes 786440 | tf_op jit(solution)/shard_map/while/body/eval_jaxpr/ppermute | solution.py:15
  505.7 7.0 %collective-permute-start.1 = (s32[256]{0:T(256)}, s32[256]{0:T(256)S(1)}, u32[]{:S(2)}, u32[]{:S(2)}) collective-permute-start(s32[256]{0:T(256)} %get-tuple-element.222), channel_id=1, source_target_pairs={{0,8},{8,16},{16,24},{24,32},{32,40},{40,48},{48,56},{56,64},{64,7... | collective-permute-start | bytes 3080 | tf_op jit(solution)/shard_map/while/body/eval_jaxpr/ppermute | solution.py:15
  527.3 7.5 %collective-permute-start.3 = (bf16[128,2,1,256]{0,3,2,1:T(8,128)(2,1)S(1)}, bf16[128,2,1,256]{0,3,2,1:T(8,128)(2,1)S(1)}, u32[]{:S(2)}, u32[]{:S(2)}) collective-permute-start(bf16[128,2,1,256]{0,3,2,1:T(8,128)(2,1)S(1)} %slice.78), channel_id=1, source_target_pairs={{8,0},{16,8},{24,16},{32,24},{40,32},{48,40},{56,48},{64,56},{72,6... | collective-permute-start | bytes 393224 | tf_op jit(solution)/shard_map/ppermute | solution.py:15
  (17 other events, 190.2 us)
Sparse Core Ops, SparseCore 0:
  518.8 165.8 reduce-scatter.1
